TPU v7x, 256 devices: a whole 4x4x8 slice. The times are simulated.
256 devices in a mesh: space: 64 (over z, x, core), inst: 4 (over y).
Axes of the slice: x: 4, y: 4, z: 8, core: 2. Of those that a mesh axis runs over, the one named last changes fastest.
Arguments:
- adjoint: float32 [8, 5, 131072], P('inst', None, 'space'), may hold values from -6 to 6
- jac_cell: float32 [8, 5, 5, 131072], P('inst', None, None, 'space'), may hold values from -2.5 to 2.5
- jac_left: float32 [8, 5, 5, 131072], P('inst', None, None, 'space'), may hold values from -2.5 to 2.5
- jac_right: float32 [8, 5, 5, 131072], P('inst', None, None, 'space'), may hold values from -2.5 to 2.5
- volume: float32 [131072], P('space'), may hold values from 0.5 to 2
- normals: float32 [3, 131072], P(None, 'space'), may hold values from -6 to 6
- surface: int32 [131072], P('space'), may hold values 0 or 1
- instance_map: int32 [8], replicated, may hold values from 0 to 7, each once
- mode_shapes: float32 [200, 3, 131072], P(None, None, 'space'), may hold values from -0.01953125 to 0.01953125
- damping: float32 [200], replicated, may hold values from 0.2 to 2
- modal_inverse: float32 [200, 200], replicated, may hold values from -2 to 3
Outputs:
- flow_residual: float32 [8, 5, 131072], P('inst', None, 'space')
- mesh_forcing: float32 [8, 3, 131072], P('inst', None, 'space')
- modal_adjoint: float32 [8, 200], P('inst')
All inputs are finite; a program needn't handle non-finite values. No bound on the sum of `surface` on one device may be relied on, other than what follows from the above.
Results may differ from a plain program's by a relative error of at most 0.000068.
Values sent between devices are 32-bit elements; how exact they have to be, the bound alone decides.
A program may use at most 64 MiB of HBM per device.

v0:
```python
import jax
import jax.numpy as jnp
from jax import lax
from jax.sharding import PartitionSpec as P


def padded_2(shard, sides, width):
    for axis, dim in sides:
        count, length = (lax.axis_size(axis), shard.shape[dim])
        up = [(i, (i + 1) % count) for i in range(count - 1)]
        down = [(j, i) for i, j in up]
        last = lax.slice_in_dim(shard, length - width, length, axis=dim)
        leading = lax.slice_in_dim(shard, 0, width, axis=dim)
        before = lax.ppermute(last, axis, up)
        after = lax.ppermute(leading, axis, down)
        shard = jnp.concatenate([before, shard, after], axis=dim)
    return shard


def coupling_matrix(instance_map):
    count = instance_map.shape[0]
    slots = instance_map.astype(jnp.float32)
    differ = slots[:, None] - slots[None, :]
    angle = jnp.pi * differ / count
    same = differ == 0
    sine = jnp.where(same, 1.0, jnp.sin(angle))
    return jnp.where(same, 0.0, 0.5 * jnp.cos(jnp.pi * differ) * jnp.cos(angle) / sine)


def shards(
    adjoint,
    jac_cell,
    jac_left,
    jac_right,
    volume,
    normals,
    surface,
    instance_map,
    mode_shapes,
    damping,
    modal_inverse,
):
    highest = lax.Precision.HIGHEST
    own_slots = adjoint.shape[0]
    modes = mode_shapes.shape[0]
    first_slot = lax.axis_index("inst") * own_slots
    coupling = coupling_matrix(instance_map)
    own_cols = lax.dynamic_slice_in_dim(coupling, first_slot, own_slots, 1)
    flow = jnp.einsum("sfec,sfc->sec", jac_cell, adjoint, precision=highest)
    from_left = jnp.einsum("sfec,sfc->sec", jac_left, adjoint, precision=highest)
    from_right = jnp.einsum("sfec,sfc->sec", jac_right, adjoint, precision=highest)
    stacked = jnp.stack([from_left, from_right])
    padded = padded_2(stacked, (("space", 3),), 1)
    flow = flow + padded[0, :, :, 2:] + padded[1, :, :, :-2]
    timed = jnp.einsum(
        "ab,aec->bec",
        own_cols,
        lax.all_gather(adjoint, "inst", axis=0, tiled=True),
        precision=highest,
    )
    flow = flow + volume[None, None, :] * timed
    walls = surface.astype(jnp.float32)
    force = (walls[None, :] * flow[:, 4, :])[:, None, :] * normals[None, :, :]
    shapes = mode_shapes.reshape(modes, -1)
    projected = lax.dot_general(
        force.reshape(own_slots, -1),
        shapes,
        (((1,), (1,)), ((), ())),
        precision=highest,
        preferred_element_type=jnp.float32,
    )
    summed = lax.psum(projected, "space")
    gathered = lax.all_gather(summed, "inst", axis=0, tiled=True)
    own_projected = lax.dynamic_slice_in_dim(gathered, first_slot, own_slots, 0)
    modal_rhs = own_projected + damping[None, :] * jnp.dot(own_cols.T, gathered, precision=highest)
    modal_adjoint = jnp.dot(modal_rhs, modal_inverse, precision=highest)
    expanded = jnp.dot(modal_adjoint, shapes, precision=highest).reshape(own_slots, 3, -1)
    mesh_forcing = walls[None, None, :] * expanded
    return (flow, mesh_forcing, modal_adjoint)


def solution(mesh):
    placed = (
        P("inst", None, "space"),
        P("inst", None, None, "space"),
        P("inst", None, None, "space"),
        P("inst", None, None, "space"),
        P("space"),
        P(None, "space"),
        P("space"),
        P(),
        P(None, None, "space"),
        P(),
        P(),
    )
    return jax.shard_map(
        shards,
        mesh=mesh,
        in_specs=placed,
        out_specs=(P("inst", None, "space"), P("inst", None, "space"), P("inst", None)),
        check_vma=False,
    )
```

profile of v0, /device:TPU:8, one launch (start us, length us, event | category | flops | bytes accessed | tf_op | source)
XLA Modules:
  0.0 175.6 jit_solution(5606615448060914393)
XLA Ops:
  0.6 0.0 copy-start
  0.6 0.0 copy-start.3
  0.7 2.1 %multiply_reduce_fusion.2 = (f32[2,2048,5]{1,0,2:T(2,128)S(1)}, f32[2,2048,5]{1,0,2:T(2,128)S(1)}, f32[2,2048,5]{1,0,2:T(2,128)S(1)}) fusion(f32[2,5,5,2048]{3,0,2,1:T(2,128)} %param.12, f32[2,2048,5]{1,0,2:T(2,128)} %bitcast.61, f32[2,5,5,2048]{3,0,2,1:T(2,128)} %param.13, f32[2,5,5,2048]{3,0,2,1:T(2,128)} %param.14), kind=kLoop, calls=%fused_computation.10 | loop fusion | flops 552960 | bytes 1556480 | tf_op jit(solution)/shard_map/sfec,sfc->sec/dot_general | solution.py:49
  2.8 0.1 pad_maximum_fusion.5
  2.9 1.7 collective-permute-start.1
  4.6 1.3 collective-permute-start
  5.9 0.9 copy.16
  6.8 13.6 %all_gather.6 = f32[8,5,2048]{2,1,0:T(8,128)S(1)} all-gather(f32[2,5,2048]{2,1,0:T(8,128)S(1)} %copy.16), channel_id=1, replica_groups=mesh['space'=64,'inst'=4] {'inst'}, dimensions={0}, use_global_device_ids=true | all-gather | bytes 409600 | tf_op jit(solution)/shard_map/all_gather | solution.py:58
  20.5 0.7 convert_element_type.6
  21.1 0.1 fusion.21
  21.3 0.7 convert_element_type.7
  22.0 0.0 collective-permute-done.1
  22.0 0.0 collective-permute-done
  22.0 1.3 fusion.10
  23.3 0.0 copy-start.2
  23.3 5.8 %convolution_bitcast_fusion = f32[2,200]{1,0:T(2,128)S(1)} fusion(f32[200,3,2048]{2,0,1:T(8,128)} %param.19, f32[3,2048]{1,0:T(4,128)} %param.16, f32[2,2048]{1,0:T(2,128)S(1)} %fusion.18), kind=kOutput, calls=%fused_computation.6 | convolution fusion | flops 29503488 | bytes 4957760 | tf_op jit(solution)/shard_map/dot_general | solution.py:65
  29.1 129.9 %psum.7 = f32[2,200]{1,0:T(2,128)S(1)} all-reduce(f32[2,200]{1,0:T(2,128)S(1)} %convolution_bitcast_fusion), channel_id=1, replica_groups=mesh['space'=64,'inst'=4] {'space'}, use_global_device_ids=true, to_apply=%region_0.1 | all-reduce | flops 400 | bytes 3200 | tf_op jit(solution)/shard_map/psum | solution.py:72
  159.1 10.7 %all-gather = f32[4,2,200]{2,1,0:T(2,128)S(1)} all-gather(f32[1,2,200]{2,1,0:T(2,128)S(1)} %bitcast.66), channel_id=1, replica_groups=mesh['space'=64,'inst'=4] {'inst'}, dimensions={0}, use_global_device_ids=true | all-gather | bytes 8000 | tf_op jit(solution)/shard_map/all_gather | solution.py:73
  169.8 0.0 copy-done.3
  169.8 0.1 fusion.6
  169.9 0.0 copy-done
  169.9 0.2 fusion.33
  170.1 5.5 %fusion.3 = f32[2,3,2048]{2,0,1:T(2,128)} fusion(f32[2048]{0:T(1024)S(1)} %convert_element_type.7, f32[2,200]{1,0:T(2,128)S(1)} %fusion.33, f32[200,3,2048]{2,0,1:T(8,128)} %param.19), kind=kOutput, calls=%fused_computation.4 | convolution fusion | flops 29503488 | bytes 4974144 | tf_op jit(solution)/shard_map/dot_general | solution.py:77
  175.6 0.0 copy-done.2
  (4 shorter events, 0.0 us)
Async XLA Ops:
  0.6 169.3 %copy-start = (f32[200,200]{1,0:T(8,128)S(1)}, f32[200,200]{1,0:T(8,128)}, u32[]{:S(2)}) copy-start(f32[200,200]{1,0:T(8,128)} %param.21) | copy-start | bytes 480004
  0.6 169.1 %copy-start.3 = (f32[200]{0:T(256)S(1)}, f32[200]{0:T(256)}, u32[]{:S(2)}) copy-start(f32[200]{0:T(256)} %param.20) | copy-start | bytes 2404
  2.9 19.1 %collective-permute-start.1 = (f32[2,2,5,1]{3,1,2,0:T(2,128)S(1)}, f32[2,2,5,1]{3,1,2,0:T(2,128)S(1)}, u32[]{:S(2)}, u32[]{:S(2)}) collective-permute-start(f32[2,2,5,1]{3,1,2,0:T(2,128)S(1)} %get-tuple-element.7), channel_id=1, source_target_pairs={{0,4},{4,8},{8,12},{12,16},{16,20},{20,24},{24,28},{28,32},{32,36}... | collective-permute-start | bytes 248 | tf_op jit(solution)/shard_map/ppermute | solution.py:14
  4.6 17.4 %collective-permute-start = (f32[2,2,5,1]{3,1,2,0:T(2,128)S(1)}, f32[2,2,5,1]{3,1,2,0:T(2,128)S(1)}, u32[]{:S(2)}, u32[]{:S(2)}) collective-permute-start(f32[2,2,5,1]{3,1,2,0:T(2,128)S(1)} %get-tuple-element.6), channel_id=1, source_target_pairs={{4,0},{8,4},{12,8},{16,12},{20,16},{24,20},{28,24},{32,28},{36,32}... | collective-permute-start | bytes 248 | tf_op jit(solution)/shard_map/ppermute | solution.py:15
  23.3 152.3 %copy-start.2 = (f32[2,5,2048]{2,0,1:T(2,128)}, f32[2,5,2048]{2,0,1:T(2,128)S(1)}, u32[]{:S(2)}) copy-start(f32[2,5,2048]{2,0,1:T(2,128)S(1)} %fusion.10) | copy-start | bytes 245764
  170.1 5.5 %copy-start.1 = (f32[2,200]{1,0:T(2,128)}, f32[2,200]{1,0:T(2,128)S(1)}, u32[]{:S(2)}) copy-start(f32[2,200]{1,0:T(2,128)S(1)} %fusion.33) | copy-start | bytes 4804
where the time goes:
time: 176 us
  blocking collectives  154 us (88%)
  matrix products  12.8 us (7%)
  other arithmetic  3.69 us (2%)
  starting transfers between devices  3.02 us (2%)
    psum x1, blocking collectives, shards(): summed = lax.psum(projected, 'space')  130 us
    all_gather x1, blocking collectives, shards(): lax.all_gather(adjoint, 'inst', axis=0, tiled=True)  13.6 us
    all_gather x1, blocking collectives, shards(): gathered = lax.all_gather(summed, 'inst', axis=0, tiled=True)  10.7 us
    dot_general x1, matrix products, shards(): lax.dot_general(force.reshape(own_slots, -1), shapes, (((1,), (1,)), ((),...  5.76 us
    dot_general x1, matrix products, shards(): jnp.dot(modal_adjoint, shapes, precision=highest).reshape(own_slots, 3, -1)  5.45 us
  transfers between devices with their start and end apart: 2, of which 0 were waited for; matrix products, arithmetic and copies ran while one was open for 1% of the time, Pallas kernels for 0%

commit v1 on v0

--- a/solution.py
+++ b/solution.py
@@ -69,7 +69,7 @@
         precision=highest,
         preferred_element_type=jnp.float32,
     )
-    summed = lax.psum(projected, "space")
+    summed = jnp.sum(lax.all_gather(projected, "space"), axis=0)
     gathered = lax.all_gather(summed, "inst", axis=0, tiled=True)
     own_projected = lax.dynamic_slice_in_dim(gathered, first_slot, own_slots, 0)
     modal_rhs = own_projected + damping[None, :] * jnp.dot(own_cols.T, gathered, precision=highest)

time: 176 us -> 102 us (0.58)
  blocking collectives: 154 us -> 80.6 us
    psum x1 -> x0, blocking collectives: 130 us -> none  [shards(): summed = lax.psum(projected, 'space')]
    all_gather x0 -> x1, blocking collectives: none -> 56.2 us  [shards(): summed = jnp.sum(lax.all_gather(projected, 'space'), axis=0)]
  transfers between devices with their start and end apart: 2 -> 2, of which waited for: 0 -> 0; matrix products, arithmetic and copies ran while one was open for 1% -> 2% of each run, Pallas kernels for 0% -> 0%
where the time goes in v1:
time: 102 us
  blocking collectives  80.6 us (79%)
  matrix products  12.8 us (13%)
  other arithmetic  3.78 us (4%)
  starting transfers between devices  3.02 us (3%)
    all_gather x1, blocking collectives, shards(): summed = jnp.sum(lax.all_gather(projected, 'space'), axis=0)  56.2 us
    all_gather x1, blocking collectives, shards(): lax.all_gather(adjoint, 'inst', axis=0, tiled=True)  13.6 us
    all_gather x1, blocking collectives, shards(): gathered = lax.all_gather(summed, 'inst', axis=0, tiled=True)  10.7 us
    dot_general x1, matrix products, shards(): lax.dot_general(force.reshape(own_slots, -1), shapes, (((1,), (1,)), ((),...  5.76 us
    dot_general x1, matrix products, shards(): jnp.dot(modal_adjoint, shapes, precision=highest).reshape(own_slots, 3, -1)  5.45 us
    dot_general x1, other arithmetic, shards(): flow = jnp.einsum('sfec,sfc->sec', jac_cell, adjoint, precision=highest)  2.12 us
  transfers between devices with their start and end apart: 2, of which 0 were waited for; matrix products, arithmetic and copies ran while one was open for 2% of the time, Pallas kernels for 0%

profile of v1, /device:TPU:8, one launch (start us, length us, event | category | flops | bytes accessed | tf_op | source)
XLA Modules:
  0.0 101.9 jit_solution(11380316839315550119)
XLA Ops:
  0.6 0.0 copy-start
  0.6 0.0 copy-start.3
  0.7 2.1 %multiply_reduce_fusion.2 = (f32[2,2048,5]{1,0,2:T(2,128)S(1)}, f32[2,2048,5]{1,0,2:T(2,128)S(1)}, f32[2,2048,5]{1,0,2:T(2,128)S(1)}) fusion(f32[2,5,5,2048]{3,0,2,1:T(2,128)} %param.12, f32[2,2048,5]{1,0,2:T(2,128)} %bitcast.62, f32[2,5,5,2048]{3,0,2,1:T(2,128)} %param.13, f32[2,5,5,2048]{3,0,2,1:T(2,128)} %param.14), kind=kLoop, calls=%fused_computation.10 | loop fusion | flops 552960 | bytes 1556480 | tf_op jit(solution)/shard_map/sfec,sfc->sec/dot_general | solution.py:49
  2.8 0.1 pad_maximum_fusion.5
  2.9 1.7 %collective-permute-start.1 = (f32[2,2,5,1]{3,1,2,0:T(2,128)S(1)}, f32[2,2,5,1]{3,1,2,0:T(2,128)S(1)}, u32[]{:S(2)}, u32[]{:S(2)}) collective-permute-start(f32[2,2,5,1]{3,1,2,0:T(2,128)S(1)} %get-tuple-element.7), channel_id=1, source_target_pairs={{0,4},{4,8},{8,12},{12,16},{16,20},{20,24},{24,28},{28,32},{32,36}... | collective-permute-start | bytes 248 | tf_op jit(solution)/shard_map/ppermute | solution.py:14
  4.6 1.3 %collective-permute-start = (f32[2,2,5,1]{3,1,2,0:T(2,128)S(1)}, f32[2,2,5,1]{3,1,2,0:T(2,128)S(1)}, u32[]{:S(2)}, u32[]{:S(2)}) collective-permute-start(f32[2,2,5,1]{3,1,2,0:T(2,128)S(1)} %get-tuple-element.6), channel_id=1, source_target_pairs={{4,0},{8,4},{12,8},{16,12},{20,16},{24,20},{28,24},{32,28},{36,32}... | collective-permute-start | bytes 248 | tf_op jit(solution)/shard_map/ppermute | solution.py:15
  5.9 0.9 copy.16
  6.8 13.6 %all_gather.12 = f32[8,5,2048]{2,1,0:T(8,128)S(1)} all-gather(f32[2,5,2048]{2,1,0:T(8,128)S(1)} %copy.16), channel_id=1, replica_groups=mesh['space'=64,'inst'=4] {'inst'}, dimensions={0}, use_global_device_ids=true | all-gather | bytes 409600 | tf_op jit(solution)/shard_map/all_gather | solution.py:58
  20.5 0.7 convert_element_type.6
  21.1 0.1 fusion.21
  21.3 0.7 convert_element_type.7
  22.0 0.0 collective-permute-done.1
  22.0 0.0 collective-permute-done
  22.0 1.3 %fusion.10 = f32[2,5,2048]{2,0,1:T(2,128)S(1)} fusion(f32[2,2,5,1]{3,1,2,0:T(2,128)S(1)} %collective-permute-done.1, f32[1,2,5,2048]{3,1,2,0:T(2,128)S(1)} %bitcast.66, f32[1,2,5,2048]{3,1,2,0:T(2,128)S(1)} %bitcast.64, f32[2,2,5,1]{3,1,2,0:T(2,128)S(1)} %collective-permute-done, f32[2,2048,5]{1,0,2:T(2,128)S(1)} %get-tuple-element.3, ...), kind=kOutput, calls=%fused_computation.15 | convolution fusion | flops 2129920 | bytes 881668 | tf_op jit(solution)/shard_map/ab,aec->bec/dot_general | solution.py:55
  23.3 0.0 copy-start.2
  23.3 5.8 %convolution_bitcast_fusion = f32[1,2,200]{2,1,0:T(2,128)S(1)} fusion(f32[200,3,2048]{2,0,1:T(8,128)} %param.19, f32[3,2048]{1,0:T(4,128)} %param.16, f32[2,2048]{1,0:T(2,128)S(1)} %fusion.18), kind=kOutput, calls=%fused_computation.6 | convolution fusion | flops 29503488 | bytes 4957760 | tf_op jit(solution)/shard_map/dot_general | solution.py:65
  29.1 56.2 %all-gather.1 = f32[64,2,200]{2,1,0:T(2,128)S(1)} all-gather(f32[1,2,200]{2,1,0:T(2,128)S(1)} %convolution_bitcast_fusion), channel_id=2, replica_groups=mesh['space'=64,'inst'=4] {'space'}, dimensions={0}, use_global_device_ids=true | all-gather | bytes 104000 | tf_op jit(solution)/shard_map/all_gather | solution.py:72
  85.3 0.1 reduce_sum.9
  85.4 10.7 %all-gather.2 = f32[4,2,200]{2,1,0:T(2,128)S(1)} all-gather(f32[1,2,200]{2,1,0:T(2,128)S(1)} %bitcast.67), channel_id=1, replica_groups=mesh['space'=64,'inst'=4] {'inst'}, dimensions={0}, use_global_device_ids=true | all-gather | bytes 8000 | tf_op jit(solution)/shard_map/all_gather | solution.py:73
  96.2 0.0 copy-done.3
  96.2 0.1 fusion.6
  96.3 0.0 copy-done
  96.3 0.2 fusion.33
  96.5 5.5 %fusion.3 = f32[2,3,2048]{2,0,1:T(2,128)} fusion(f32[2048]{0:T(1024)S(1)} %convert_element_type.7, f32[2,200]{1,0:T(2,128)S(1)} %fusion.33, f32[200,3,2048]{2,0,1:T(8,128)} %param.19), kind=kOutput, calls=%fused_computation.4 | convolution fusion | flops 29503488 | bytes 4974144 | tf_op jit(solution)/shard_map/dot_general | solution.py:77
  (5 shorter events, 0.0 us)
Async XLA Ops:
  0.6 95.7 %copy-start = (f32[200,200]{1,0:T(8,128)S(1)}, f32[200,200]{1,0:T(8,128)}, u32[]{:S(2)}) copy-start(f32[200,200]{1,0:T(8,128)} %param.21) | copy-start | bytes 480004
  0.6 95.5 %copy-start.3 = (f32[200]{0:T(256)S(1)}, f32[200]{0:T(256)}, u32[]{:S(2)}) copy-start(f32[200]{0:T(256)} %param.20) | copy-start | bytes 2404
  2.9 19.1 %collective-permute-start.1 = (f32[2,2,5,1]{3,1,2,0:T(2,128)S(1)}, f32[2,2,5,1]{3,1,2,0:T(2,128)S(1)}, u32[]{:S(2)}, u32[]{:S(2)}) collective-permute-start(f32[2,2,5,1]{3,1,2,0:T(2,128)S(1)} %get-tuple-element.7), channel_id=1, source_target_pairs={{0,4},{4,8},{8,12},{12,16},{16,20},{20,24},{24,28},{28,32},{32,36}... | collective-permute-start | bytes 248 | tf_op jit(solution)/shard_map/ppermute | solution.py:14
  4.6 17.4 %collective-permute-start = (f32[2,2,5,1]{3,1,2,0:T(2,128)S(1)}, f32[2,2,5,1]{3,1,2,0:T(2,128)S(1)}, u32[]{:S(2)}, u32[]{:S(2)}) collective-permute-start(f32[2,2,5,1]{3,1,2,0:T(2,128)S(1)} %get-tuple-element.6), channel_id=1, source_target_pairs={{4,0},{8,4},{12,8},{16,12},{20,16},{24,20},{28,24},{32,28},{36,32}... | collective-permute-start | bytes 248 | tf_op jit(solution)/shard_map/ppermute | solution.py:15
  23.3 78.6 %copy-start.2 = (f32[2,5,2048]{2,0,1:T(2,128)}, f32[2,5,2048]{2,0,1:T(2,128)S(1)}, u32[]{:S(2)}) copy-start(f32[2,5,2048]{2,0,1:T(2,128)S(1)} %fusion.10) | copy-start | bytes 245764
  96.5 5.5 %copy-start.1 = (f32[2,200]{1,0:T(2,128)}, f32[2,200]{1,0:T(2,128)S(1)}, u32[]{:S(2)}) copy-start(f32[2,200]{1,0:T(2,128)S(1)} %fusion.33) | copy-start | bytes 4804
